TPU v7x, 256 devices: a whole 4x4x8 slice. The times are simulated.
256 devices in a mesh: tok: 64 (over z, x, core), grp: 4 (over y).
Axes of the slice: x: 4, y: 4, z: 8, core: 2. Of those that a mesh axis runs over, the one named last changes fastest.
Arguments:
- inputs: float32 [4, 8192, 1536], P('grp', 'tok'), may hold values from -6 to 6
- queries: bfloat16 [4, 8192, 1536], P('grp', 'tok'), may hold values from -100 to 100
- keys: bfloat16 [4, 8192, 256], P('grp', 'tok'), may hold values from -6 to 6
- values: bfloat16 [4, 8192, 256], P('grp', 'tok'), may hold values from -6 to 6
- prefix_keys: bfloat16 [2048, 256], P(('tok', 'grp')), may hold values from -7 to 7
- prefix_values: bfloat16 [2048, 256], P(('tok', 'grp')), may hold values from -6 to 6
- lengths: int32 [4, 16], replicated, may hold values from 1 to 4224, 8192 in all within a row
- out_weight: bfloat16 [1536, 1536], replicated, may hold values from -0.5 to 0.5
- norm_gain: float32 [1536], replicated, may hold values from 0.25 to 1.75
- router_weight: bfloat16 [1536, 32], replicated, may hold values from -0.15625 to 0.15625
- routes: int32 [4, 8192, 4], P('grp', 'tok'), may hold values from 0 to 31, all different within a row; in each aligned block of 128 rows (0 to 127, 128 to 255, ..., all dimensions but the last counted through in order) at most 24 rows name the same one
- expert_gate: bfloat16 [64, 1536, 384], P('tok'), may hold values from -0.15625 to 0.15625
- expert_up: bfloat16 [64, 1536, 384], P('tok'), may hold values from -0.15625 to 0.15625
- expert_down: bfloat16 [64, 384, 1536], P('tok'), may hold values from -0.21875 to 0.21875
Outputs:
- layer_out: float32 [4, 8192, 1536], P('grp', 'tok')
Inputs may be any that keep to these rules, and one draw needn't show every extreme that they name: Row g holds the suffix lengths of the 16 requests of group g, in order; they sum to 8192, and the longest is exactly 4224. `routes`: each token names 4 different experts; of one device's 128 tokens no more than 24 name one expert, and in every draw some expert is named by exactly 24 of them.
All inputs are finite; a program needn't handle non-finite values.
Results may differ from a plain program's by a relative error of at most 0.0055.
Values may be sent and summed in bfloat16 or wider, within the bound.
A program may use at most 192 MiB of HBM per device.

v0:
```python
import math
import jax
import jax.numpy as jnp
from jax import lax
from jax.sharding import PartitionSpec as P

HEADS = 12
KVH = 2
HD = 128
EXPERTS = 32
TOP = 4
CAP = 24
NEGATIVE = -1e30


def absorb(running, key_piece, value_piece, valid, query_heads):
    running_max, denominator, numerator = running
    key_count = key_piece.shape[0]
    key_heads = key_piece.reshape(key_count, KVH, HD)
    value_heads = value_piece.reshape(key_count, KVH, HD)
    scores = jnp.einsum(
        "tgrd,kgd->grtk", query_heads, key_heads, preferred_element_type=jnp.float32
    ) * (1.0 / math.sqrt(HD))
    if valid is None:
        masked = scores
    else:
        masked = jnp.where(valid[None, None], scores, NEGATIVE)
    new_max = jnp.maximum(running_max, jnp.max(masked, axis=-1))
    factor = jnp.exp(running_max - new_max)
    weights = jnp.exp(masked - new_max[..., None])
    if valid is not None:
        weights = jnp.where(valid[None, None], weights, 0.0)
    denominator = denominator * factor + jnp.sum(weights, axis=-1)
    numerator = numerator * factor[..., None] + jnp.einsum(
        "grtk,kgd->grtd",
        weights.astype(jnp.bfloat16),
        value_heads,
        preferred_element_type=jnp.float32,
    )
    return (new_max, denominator, numerator)


def local(
    inputs,
    queries,
    keys,
    values,
    prefix_keys,
    prefix_values,
    lengths,
    out_weight,
    norm_gain,
    router_weight,
    routes,
    expert_gate,
    expert_up,
    expert_down,
):
    tok_rows = queries.shape[1]
    model_width = out_weight.shape[1]
    repeat = HEADS // KVH
    query_heads = queries[0].reshape(tok_rows, KVH, repeat, HD)
    device = lax.axis_index("tok")
    positions = device * tok_rows + jnp.arange(tok_rows, dtype=jnp.int32)
    row_lengths = lax.dynamic_index_in_dim(lengths, lax.axis_index("grp"), 0, keepdims=False)
    request_ends = jnp.cumsum(row_lengths)
    starts = jnp.max(
        jnp.where(request_ends[None, :] <= positions[:, None], request_ends[None, :], 0), axis=1
    )
    softmax_state = (
        jnp.full((KVH, repeat, tok_rows), NEGATIVE, jnp.float32),
        jnp.zeros((KVH, repeat, tok_rows), jnp.float32),
        jnp.zeros((KVH, repeat, tok_rows, HD), jnp.float32),
    )
    shard_pair = (
        lax.all_gather(prefix_keys, ("tok", "grp"), axis=0, tiled=True),
        lax.all_gather(prefix_values, ("tok", "grp"), axis=0, tiled=True),
    )
    softmax_state = absorb(softmax_state, shard_pair[0], shard_pair[1], None, query_heads)
    own_keys = keys[0]
    own_values = values[0]
    shard_pair = (
        lax.all_gather(own_keys, "tok", axis=0, tiled=True),
        lax.all_gather(own_values, "tok", axis=0, tiled=True),
    )
    key_positions = jnp.arange(shard_pair[0].shape[0], dtype=jnp.int32)
    softmax_state = absorb(
        softmax_state,
        shard_pair[0],
        shard_pair[1],
        (key_positions[None, :] >= starts[:, None])
        & (key_positions[None, :] <= positions[:, None]),
        query_heads,
    )
    attended = (softmax_state[2] / softmax_state[1][..., None]).astype(jnp.bfloat16)
    attended = attended.transpose(2, 0, 1, 3).reshape(tok_rows, HEADS * HD)
    residual = inputs[0] + jnp.dot(attended, out_weight, preferred_element_type=jnp.float32)
    normed = (
        residual
        * lax.rsqrt(jnp.mean(residual * residual, axis=-1, keepdims=True) + 1e-06)
        * norm_gain
    ).astype(jnp.bfloat16)
    logits = jnp.dot(normed, router_weight, preferred_element_type=jnp.float32)
    token_routes = routes[0]
    sigmoids = jax.nn.sigmoid(jnp.take_along_axis(logits, token_routes, axis=1))
    gate_weights = sigmoids / jnp.sum(sigmoids, axis=1, keepdims=True)
    pair_experts = token_routes.reshape(-1)
    onehot = (pair_experts[:, None] == jnp.arange(EXPERTS, dtype=jnp.int32)[None, :]).astype(
        jnp.int32
    )
    slot_index = jnp.sum(jnp.cumsum(onehot, axis=0) * onehot, axis=1) - 1
    targets = pair_experts * CAP + slot_index
    buffer = (
        jnp.zeros((EXPERTS * CAP, model_width), jnp.bfloat16)
        .at[targets]
        .set(jnp.repeat(normed, TOP, axis=0))
    )
    local_slices = expert_gate.shape[0]
    tok_count = lax.axis_size("tok")
    split_count = local_slices * tok_count // EXPERTS
    outgoing = jnp.repeat(buffer.reshape(EXPERTS, CAP, model_width), split_count, axis=0).reshape(
        tok_count, local_slices, CAP, model_width
    )
    weight_sets = (expert_gate[:, None], expert_up[:, None], expert_down[:, None])
    arrived = lax.all_to_all(outgoing, "tok", split_axis=0, concat_axis=0, tiled=True)
    sources = arrived.shape[0]
    slot_count = arrived.shape[2]
    slot_rows = arrived[:, 0].reshape(sources * slot_count, model_width)
    gated = jax.nn.relu(
        jnp.dot(slot_rows, weight_sets[0][0, 0], preferred_element_type=jnp.float32)
    )
    hidden = (
        gated * jnp.dot(slot_rows, weight_sets[1][0, 0], preferred_element_type=jnp.float32)
    ).astype(jnp.bfloat16)
    part_out = jnp.dot(hidden, weight_sets[2][0, 0], preferred_element_type=jnp.float32).astype(
        jnp.bfloat16
    )
    total = lax.optimization_barrier(part_out).astype(jnp.float32)
    results = [total.astype(jnp.bfloat16).reshape(sources, slot_count, model_width)]
    computed = jnp.stack(results, axis=1)
    returned = lax.all_to_all(computed, "tok", split_axis=0, concat_axis=0, tiled=True)
    summed = jnp.sum(
        returned.reshape(EXPERTS, split_count, CAP, model_width).astype(jnp.float32), axis=1
    ).reshape(EXPERTS * CAP, model_width)
    expert_out = lax.optimization_barrier(summed.astype(jnp.bfloat16)).astype(jnp.float32)
    combined = jnp.sum(
        expert_out[targets].reshape(tok_rows, TOP, model_width) * gate_weights[:, :, None], axis=1
    )
    return (residual + combined)[None]


def solution(mesh):
    placed = (
        P("grp", "tok", None),
        P("grp", "tok", None),
        P("grp", "tok", None),
        P("grp", "tok", None),
        P(("tok", "grp"), None),
        P(("tok", "grp"), None),
        P(),
        P(),
        P(),
        P(),
        P("grp", "tok", None),
        P("tok", None, None),
        P("tok", None, None),
        P("tok", None, None),
    )
    return jax.shard_map(
        local, mesh=mesh, in_specs=placed, out_specs=P("grp", "tok", None), check_vma=False
    )
```

profile of v0, /device:TPU:8, one launch (start us, length us, event | category | flops | bytes accessed | tf_op | source)
XLA Modules:
  0.0 691.7 jit_solution(8346470615721139849)
XLA Ops:
  6.5 0.7 all-gather.7.cloned.1.call-update
  7.3 0.0 all-gather.9.cloned.1.call-start
  7.3 0.7 all-gather.9.cloned.1.call-update
  8.0 0.0 all-gather.11.cloned.1.call-start
  8.1 1.6 copy.86
  9.6 0.0 all-gather.11.cloned.1.call-update
  9.6 0.0 all-gather.13.cloned.1.call-start
  9.7 0.5 all-gather.13.cloned.1.call-update
  10.2 0.8 copy.92
  11.0 0.1 eq.29
  11.1 0.1 eq.25
  11.2 0.7 broadcast_multiply_fusion
  11.9 0.7 dynamic-slice_bitcast_fusion
  12.6 0.1 copy.85
  12.7 0.1 reduce.1
  12.9 0.1 select_reduce_fusion
  12.9 1.0 fusion.11
  13.9 1.9 copy.80
  15.8 1.2 reduce-window.19
  17.0 0.2 slice_reduce_fusion
  17.3 0.1 fusion.42
  17.4 0.1 copy.91
  17.5 0.1 mul.105
  17.6 99.3 %all-gather.7.cloned.1.call-done = bf16[2048,256]{1,0:T(8,128)(2,1)} async-done(((bf16[8,256]{1,0:T(8,128)(2,1)}), bf16[2048,256]{1,0:T(8,128)(2,1)}) %all-gather.7.cloned.1.call-update) | async-done | bytes 1048592 | tf_op jit(solution)/shard_map/all_gather | solution.py:76
  116.9 1.5 copy.79
  118.4 7.3 %bitcast_reduce_fusion = (f32[2,6,128]{2,1,0:T(8,128)S(1)}, f32[2,2048,128,6]{2,1,3,0:T(8,128)}) fusion(bf16[2048,2,128,1]{0,2,3,1:T(8,128)(2,1)S(1)} %bitcast.168, bf16[128,2,6,128]{0,3,2,1:T(8,128)(2,1)} %bitcast.171), kind=kOutput, calls=%fused_computation.11 | convolution fusion | flops 811596288 | bytes 14030848 | tf_op jit(solution)/shard_map/tgrd,kgd->grtk/dot_general | solution.py:21
  125.7 96.9 %all-gather.9.cloned.1.call-done = bf16[2048,256]{1,0:T(8,128)(2,1)} async-done(((bf16[8,256]{1,0:T(8,128)(2,1)}), bf16[2048,256]{1,0:T(8,128)(2,1)}) %all-gather.9.cloned.1.call-update) | async-done | bytes 1048592 | tf_op jit(solution)/shard_map/all_gather | solution.py:77
  222.6 1.5 copy.83
  224.1 76.4 %all-gather.11.cloned.1.call-done = bf16[1,8192,256]{1,2,0:T(8,128)(2,1)} async-done(((bf16[1,128,256]{1,2,0:T(8,128)(2,1)}), bf16[1,8192,256]{1,2,0:T(8,128)(2,1)}) %all-gather.11.cloned.1.call-update) | async-done | bytes 4194320 | tf_op jit(solution)/shard_map/all_gather | solution.py:83
  300.4 21.5 %fusion = (f32[2,6,128]{2,1,0:T(8,128)S(1)}, f32[2,8192,128,6]{2,1,3,0:T(8,128)}) fusion(pred[128,8192]{0,1:T(8,128)(4,1)S(1)} %fusion.11, bf16[8192,2,128,1]{0,2,3,1:T(8,128)(2,1)} %bitcast.177, bf16[128,2,6,128]{0,3,2,1:T(8,128)(2,1)} %bitcast.172), kind=kOutput, calls=%fused_computation.5 | convolution fusion | flops 3258972672 | bytes 55973888 | tf_op jit(solution)/shard_map/tgrd,kgd->grtk/dot_general | solution.py:21
  321.9 6.8 fusion.7
  328.8 23.4 %fusion.1 = f32[2,6,128]{2,1,0:T(8,128)S(1)} fusion(f32[2,8192,128,6]{2,1,3,0:T(8,128)} %get-tuple-element.11, f32[2,6,128]{2,1,0:T(8,128)S(1)} %get-tuple-element.8, pred[128,8192]{0,1:T(8,128)(4,1)S(1)} %fusion.11), kind=kLoop, calls=%fused_computation.6 | loop fusion | flops 62913024 | bytes 51392512 | tf_op jit(solution)/shard_map/reduce_sum | solution.py:33
  352.2 3.3 fusion.25
  355.5 26.0 %all-gather.13.cloned.1.call-done = bf16[1,8192,256]{2,1,0:T(8,128)(2,1)} async-done(((bf16[1,128,256]{2,1,0:T(8,128)(2,1)}), bf16[1,8192,256]{2,1,0:T(8,128)(2,1)}) %all-gather.13.cloned.1.call-update) | async-done | bytes 4194320 | tf_op jit(solution)/shard_map/all_gather | solution.py:84
  381.5 6.3 copy.89
  387.8 20.6 %fusion.36 = bf16[128,2,6,128]{0,3,2,1:T(8,128)(2,1)S(1)} fusion(f32[128,2,6,128]{0,3,2,1:T(8,128)} %fusion.25, bf16[8192,2,128,1]{0,2,3,1:T(8,128)(2,1)} %bitcast.169, f32[2,8192,128,6]{2,1,3,0:T(8,128)} %get-tuple-element.11, f32[2,6,128]{2,1,0:T(8,128)S(1)} %get-tuple-element.8, pred[128,8192]{0,1:T(8,128)(4,1)S(1)} %fusion.11, ...), kind=kOutput, calls=%fused_computation.37 | convolution fusion | flops 3284729856 | bytes 56766464 | tf_op jit(solution)/shard_map/grtk,kgd->grtd/dot_general | solution.py:34
  408.4 0.0 copy-start.9
  408.5 3.2 multiply_reduce_fusion.1
  411.7 0.9 copy-done.1
  412.6 0.1 multiply_convert_fusion
  412.7 0.7 copy-done.4
  413.5 0.4 broadcast_in_dim.82
  413.9 1.4 reshape.282
  415.2 4.6 scatter_custom_fusion
  419.8 0.4 broadcast_in_dim.83
  420.2 113.8 %all_to_all.10 = bf16[64,1,24,1536]{3,2,1,0:T(8,128)(2,1)S(1)} all-to-all(bf16[64,1,24,1536]{3,2,1,0:T(8,128)(2,1)S(1)} %bitcast.162), channel_id=1, replica_groups=mesh['tok'=64,'grp'=4] {'tok'}, dimensions={0} | all-to-all | bytes 9437184 | tf_op jit(solution)/shard_map/all_to_all | solution.py:125
  534.0 2.2 copy-done.3
  536.2 4.0 convolution_maximum_fusion
  540.2 8.6 %convolution_convert_fusion = bf16[1536,1536]{1,0:T(8,128)(2,1)} fusion(bf16[1,384,1536]{2,1,0:T(8,128)(2,1)S(1)} %copy-done, f32[1536,384]{1,0:T(8,128)} %convolution_maximum_fusion, bf16[1536,1536]{1,0:T(8,128)(2,1)} %bitcast.167, bf16[1,1536,384]{2,1,0:T(8,128)(2,1)S(1)} %copy-done.11), kind=kOutput, calls=%fused_computation.15 | convolution fusion | flops 3627417600 | bytes 14155776 | tf_op jit(solution)/shard_map/dot_general | solution.py:135
  548.8 6.1 all-to-all-start.1
  554.9 0.1 copy.96
  555.1 0.1 reshape.272
  555.2 0.2 fusion.57
  555.4 3.8 gather_fusion.1
  559.2 0.1 reshape.275
  559.3 0.1 copy.97
  559.4 0.1 copy.98
  559.5 102.9 %all-to-all-done.1 = bf16[64,1,24,1536]{3,2,1,0:T(8,128)(2,1)} async-done(((bf16[64,1,24,1536]{3,2,1,0:T(8,128)(2,1)}), bf16[64,1,24,1536]{3,2,1,0:T(8,128)(2,1)}, u32[]{:S(2)}, u32[]{:S(2)}) %all-to-all-start.1) | async-done | bytes 4718624 | tf_op jit(solution)/shard_map/all_to_all | solution.py:141
  662.5 3.0 bitcast_reduce_fusion.1
  665.5 2.8 convert_element_type.56
  668.3 6.9 gather_fusion
  675.2 4.9 reshape.263
  680.0 4.2 multiply_reduce_fusion
  684.2 1.0 add_bitcast_fusion
  (42 shorter events, 0.3 us)
Async XLA Ops:
  6.5 533.6 %copy-start = (bf16[1,384,1536]{2,1,0:T(8,128)(2,1)S(1)}, bf16[1,384,1536]{2,1,0:T(8,128)(2,1)}, u32[]{:S(2)}) copy-start(bf16[1,384,1536]{2,1,0:T(8,128)(2,1)} %param.27) | copy-start | bytes 3538948
  6.5 110.3 %all-gather.7.cloned.1.call-start = ((), (), s32[]{:S(2)}) async-start(), calls=%async_computation.2 | async-start | bytes 1052672 | tf_op jit(solution)/shard_map/all_gather | solution.py:76
  7.3 215.3 %all-gather.9.cloned.1.call-start = ((), (), s32[]{:S(2)}) async-start(), calls=%async_computation.3 | async-start | bytes 1052672 | tf_op jit(solution)/shard_map/all_gather | solution.py:77
  8.0 292.4 %all-gather.11.cloned.1.call-start = ((), (), s32[]{:S(2)}) async-start(), calls=%async_computation.4 | async-start | bytes 4259840 | tf_op jit(solution)/shard_map/all_gather | solution.py:83
  9.6 371.8 %all-gather.13.cloned.1.call-start = ((), (), s32[]{:S(2)}) async-start(), calls=%async_computation.5 | async-start | bytes 4259840 | tf_op jit(solution)/shard_map/all_gather | solution.py:84
  321.9 30.2 %slice-start = ((s8[12582912]{0:T(1024)(128)(4,1)}), s8[4194304]{0:T(1024)(128)(4,1)S(1)}, s32[]{:S(2)}) async-start(s8[12582912]{0:T(1024)(128)(4,1)} %bitcast.160), calls=%async_computation.6 | async-start | bytes 8388608
  328.7 23.4 %slice-start.1 = ((s8[12582912]{0:T(1024)(128)(4,1)}), s8[4194304]{0:T(1024)(128)(4,1)S(1)}, s32[]{:S(2)}) async-start(s8[12582912]{0:T(1024)(128)(4,1)} %bitcast.160), calls=%async_computation.7 | async-start | bytes 8388608
  328.7 23.4 %slice-start.2 = ((s8[12582912]{0:T(1024)(128)(4,1)}), s8[4194304]{0:T(1024)(128)(4,1)S(1)}, s32[]{:S(2)}) async-start(s8[12582912]{0:T(1024)(128)(4,1)} %bitcast.160), calls=%async_computation.8 | async-start | bytes 8388608
  387.8 20.6 %copy-start.6 = (f32[1,128,1536]{2,1,0:T(8,128)S(1)}, f32[1,128,1536]{2,1,0:T(8,128)}, u32[]{:S(2)}) copy-start(f32[1,128,1536]{2,1,0:T(8,128)} %param.14) | copy-start | bytes 2359300
  408.4 4.1 copy-start.9
  411.7 0.9 copy-start.1
  412.7 0.7 copy-start.4
  420.2 115.9 %copy-start.10 = (bf16[1,1536,384]{2,1,0:T(8,128)(2,1)S(1)}, bf16[1,1536,384]{2,1,0:T(8,128)(2,1)}, u32[]{:S(2)}) copy-start(bf16[1,1536,384]{2,1,0:T(8,128)(2,1)} %param.25) | copy-start | bytes 3538948
  534.0 2.2 copy-start.3
  536.2 4.0 copy-start.11
  548.8 6.1 copy-start.8
  548.8 6.4 copy-start.5
  548.8 6.4 copy-start.7
  548.8 113.7 %all-to-all-start.1 = ((bf16[64,1,24,1536]{3,2,1,0:T(8,128)(2,1)}), bf16[64,1,24,1536]{3,2,1,0:T(8,128)(2,1)}, u32[]{:S(2)}, u32[]{:S(2)}) async-start(bf16[64,1,24,1536]{3,2,1,0:T(8,128)(2,1)} %bitcast.165), calls=%async_computation.1 | async-start | bytes 9437184 | tf_op jit(solution)/shard_map/all_to_all | solution.py:141
  675.2 9.0 %copy-start.2 = (f32[128,1536]{1,0:T(8,128)S(1)}, f32[128,1536]{1,0:T(8,128)}, u32[]{:S(2)}) copy-start(f32[128,1536]{1,0:T(8,128)} %copy-done.1) | copy-start | bytes 2359300
Sparse Core Ops, SparseCore 0:
  11.1 105.7 all-gather.6
  120.6 101.9 all-gather.8
  225.2 75.1 all-gather.10
  303.1 78.3 all-gather.12
where the time goes:
time: 693 us; the launch traced here: 692 us
  waiting for transfers between devices  403 us (58%)
  blocking collectives  114 us (16%)
  matrix products  68.7 us (10%)
  other arithmetic  44.6 us (6%)
  local copies, waits for them, and re-layouts  41.6 us (6%)
  between operations  13.5 us (2%)
    all_to_all x1, blocking collectives, local(): lax.all_to_all(outgoing, 'tok', split_axis=0, concat_axis=0, tiled=True)  114 us
    all_to_all x1, waiting for transfers between devices, local(): lax.all_to_all(computed, 'tok', split_axis=0, concat_axis=0, tiled=True)  103 us
    all_gather x1, waiting for transfers between devices, local(): lax.all_gather(prefix_keys, ('tok', 'grp'), axis=0, tiled=True)  99.3 us
    all_gather x1, waiting for transfers between devices, local(): lax.all_gather(prefix_values, ('tok', 'grp'), axis=0, tiled=True)  96.9 us
    all_gather x1, waiting for transfers between devices, local(): lax.all_gather(own_keys, 'tok', axis=0, tiled=True)  76.4 us
    reduce_sum x2, other arithmetic, absorb(): denominator = denominator * factor + jnp.sum(weights, axis=-1)  30.2 us
    dot_general x2, matrix products, absorb(): jnp.einsum('tgrd,kgd->grtk', query_heads, key_heads, preferred_element_ty...  28.8 us
    all_gather x1, waiting for transfers between devices, local(): lax.all_gather(own_values, 'tok', axis=0, tiled=True)  26 us
  transfers between devices with their start and end apart: 5, of which 5 were waited for; matrix products, arithmetic and copies ran while one was open for 11% of the time, Pallas kernels for 0%

commit v1 on v0

--- a/solution.py
+++ b/solution.py
@@ -80,7 +80,9 @@
     own_keys = keys[0]
     own_values = values[0]
     shard_pair = (
-        lax.all_gather(own_keys, "tok", axis=0, tiled=True),
+        jnp.concatenate(
+            lax.all_to_all(jnp.stack([own_keys] * lax.axis_size("tok")), "tok", 0, 0), axis=0
+        ),
         lax.all_gather(own_values, "tok", axis=0, tiled=True),
     )
     key_positions = jnp.arange(shard_pair[0].shape[0], dtype=jnp.int32)

time: 693 us -> 647 us (0.934); the launches traced: 692 us -> 637 us
  waiting for transfers between devices: 403 us -> 320 us
  local copies, waits for them, and re-layouts: 41.6 us -> 57.6 us
  starting transfers between devices: 6.25 us -> 18.8 us
    all_gather x1 -> x0, waiting for transfers between devices: 76.4 us -> none  [local(): lax.all_gather(own_keys, 'tok', axis=0, tiled=True)]
    all_gather x1, waiting for transfers between devices: 26 us -> 1.72 us  [local(): lax.all_gather(own_values, 'tok', axis=0, tiled=True)]
    all_to_all x0 -> x1, starting transfers between devices: none -> 12.3 us  [local(): lax.all_to_all(jnp.stack([own_keys] * lax.axis_size('tok')), 'tok', 0, 0)]
    another operation x3 -> x6, local copies, waits for them, and re-layouts: 0.78 us -> 12.2 us  [the longest x1 7.36 us: absorb(): key_heads = key_piece.reshape(key_count, KVH, HD)]
    all_gather x1, waiting for transfers between devices: 99.3 us -> 109 us  [local(): lax.all_gather(prefix_keys, ('tok', 'grp'), axis=0, tiled=True)]
    all_gather x1, waiting for transfers between devices: 96.9 us -> 104 us  [local(): lax.all_gather(prefix_values, ('tok', 'grp'), axis=0, tiled=True)]
  transfers between devices with their start and end apart: 5 -> 5, of which waited for: 5 -> 4; matrix products, arithmetic and copies ran while one was open for 11% -> 14% of each run, Pallas kernels for 0% -> 0%
where the time goes in v1:
time: 647 us; the launch traced here: 637 us
  waiting for transfers between devices  320 us (49%)
  blocking collectives  114 us (18%)
  matrix products  68.6 us (11%)
  local copies, waits for them, and re-layouts  57.6 us (9%)
  other arithmetic  44.3 us (7%)
  starting transfers between devices  18.8 us (3%)
  between operations  13.7 us (2%)
    all_to_all x1, blocking collectives, local(): lax.all_to_all(outgoing, 'tok', split_axis=0, concat_axis=0, tiled=True)  114 us
    all_gather x1, waiting for transfers between devices, local(): lax.all_gather(prefix_keys, ('tok', 'grp'), axis=0, tiled=True)  109 us
    all_gather x1, waiting for transfers between devices, local(): lax.all_gather(prefix_values, ('tok', 'grp'), axis=0, tiled=True)  104 us
    all_to_all x1, waiting for transfers between devices, local(): lax.all_to_all(computed, 'tok', split_axis=0, concat_axis=0, tiled=True)  103 us
    reduce_sum x2, other arithmetic, absorb(): denominator = denominator * factor + jnp.sum(weights, axis=-1)  30.5 us
    dot_general x2, matrix products, absorb(): jnp.einsum('tgrd,kgd->grtk', query_heads, key_heads, preferred_element_ty...  28.7 us
    dot_general x2, matrix products, absorb(): jnp.einsum('grtk,kgd->grtd', weights.astype(jnp.bfloat16), value_heads, p...  23.9 us
  transfers between devices with their start and end apart: 5, of which 4 were waited for; matrix products, arithmetic and copies ran while one was open for 14% of the time, Pallas kernels for 0%

profile of v1, /device:TPU:8, one launch (start us, length us, event | category | flops | bytes accessed | tf_op | source)
XLA Modules:
  0.0 636.9 jit_solution(533115357203324467)
XLA Ops:
  6.5 1.0 copy.88
  7.6 3.0 stack.3
  10.6 12.3 %all-to-all-start = ((bf16[64,128,256]{1,2,0:T(8,128)(2,1)}), bf16[64,128,256]{1,2,0:T(8,128)(2,1)}, u32[]{:S(2)}, u32[]{:S(2)}) async-start(bf16[64,128,256]{1,2,0:T(8,128)(2,1)} %stack.3), calls=%async_computation | async-start | bytes 8388608 | tf_op jit(solution)/shard_map/all_to_all | solution.py:84
  22.9 0.0 all-gather.5.cloned.1.call-start
  23.0 0.7 all-gather.5.cloned.1.call-update
  23.7 0.0 all-gather.7.cloned.1.call-start
  23.7 0.7 all-gather.7.cloned.1.call-update
  24.4 0.0 all-gather.9.cloned.1.call-start
  24.5 0.7 all-gather.9.cloned.1.call-update
  25.2 0.1 copy.95
  25.3 0.1 eq.29
  25.4 0.1 eq.25
  25.5 0.7 dynamic-slice_bitcast_fusion
  26.2 0.1 copy.87
  26.3 0.1 reduce.1
  26.4 0.9 copy.82
  27.4 1.2 reduce-window.19
  28.5 0.2 slice_reduce_fusion
  28.8 0.1 copy.94
  28.9 0.1 mul.105
  29.0 0.1 select_reduce_fusion
  29.1 0.1 fusion.44
  29.3 1.0 fusion.13
  30.2 108.7 %all-gather.5.cloned.1.call-done = bf16[2048,256]{1,0:T(8,128)(2,1)} async-done(((bf16[8,256]{1,0:T(8,128)(2,1)}), bf16[2048,256]{1,0:T(8,128)(2,1)}) %all-gather.5.cloned.1.call-update) | async-done | bytes 1048592 | tf_op jit(solution)/shard_map/all_gather | solution.py:76
  138.9 1.5 copy.81
  140.4 104.4 %all-gather.7.cloned.1.call-done = bf16[2048,256]{1,0:T(8,128)(2,1)} async-done(((bf16[8,256]{1,0:T(8,128)(2,1)}), bf16[2048,256]{1,0:T(8,128)(2,1)}) %all-gather.7.cloned.1.call-update) | async-done | bytes 1048592 | tf_op jit(solution)/shard_map/all_gather | solution.py:77
  244.7 2.3 copy.85
  247.0 7.3 %bitcast_reduce_fusion = (f32[2,6,128]{2,1,0:T(8,128)S(1)}, f32[2,2048,128,6]{2,1,3,0:T(8,128)}) fusion(bf16[2048,2,128,1]{0,2,3,1:T(8,128)(2,1)S(1)} %bitcast.172, bf16[128,2,6,128]{0,3,2,1:T(8,128)(2,1)} %bitcast.175), kind=kOutput, calls=%fused_computation.11 | convolution fusion | flops 811596288 | bytes 14030848 | tf_op jit(solution)/shard_map/tgrd,kgd->grtk/dot_general | solution.py:21
  254.3 6.9 %copy.89 = bf16[64,128,256]{1,0,2:T(8,128)(2,1)} copy(bf16[64,128,256]{1,2,0:T(8,128)(2,1)} %all-to-all-done) | data formatting | bytes 8388608 | tf_op jit(solution)/shard_map/all_to_all | solution.py:84
  261.2 7.4 %reshape_reshape.6 = bf16[8192,2,128]{0,2,1:T(8,128)(2,1)} reshape(bf16[64,128,256]{1,0,2:T(8,128)(2,1)} %copy.89) | data formatting | bytes 8388608 | tf_op jit(solution)/shard_map/reshape;reshape | solution.py:19
  268.5 21.4 %fusion = (f32[2,6,128]{2,1,0:T(8,128)S(1)}, f32[2,8192,128,6]{2,1,3,0:T(8,128)}) fusion(pred[128,8192]{0,1:T(8,128)(4,1)S(1)} %fusion.13, bf16[128,2,6,128]{0,3,2,1:T(8,128)(2,1)S(1)} %bitcast.176, bf16[8192,2,128]{0,2,1:T(8,128)(2,1)} %reshape_reshape.6), kind=kOutput, calls=%fused_computation.5 | convolution fusion | flops 3258972672 | bytes 55973888 | tf_op jit(solution)/shard_map/tgrd,kgd->grtk/dot_general | solution.py:21
  289.9 6.8 %fusion.7 = f32[2,6,128]{2,1,0:T(8,128)S(1)} fusion(f32[2,2048,128,6]{2,1,3,0:T(8,128)} %get-tuple-element.13, f32[2,6,128]{2,1,0:T(8,128)S(1)} %get-tuple-element.9), kind=kLoop, calls=%fused_computation.13 | loop fusion | flops 9435648 | bytes 12595200 | tf_op jit(solution)/shard_map/reduce_sum | solution.py:33
  296.8 23.8 %fusion.1 = f32[2,6,128]{2,1,0:T(8,128)S(1)} fusion(f32[2,8192,128,6]{2,1,3,0:T(8,128)} %get-tuple-element.11, f32[2,6,128]{2,1,0:T(8,128)S(1)} %get-tuple-element.8, pred[128,8192]{0,1:T(8,128)(4,1)S(1)} %fusion.13), kind=kLoop, calls=%fused_computation.6 | loop fusion | flops 62913024 | bytes 51392512 | tf_op jit(solution)/shard_map/reduce_sum | solution.py:33
  320.6 3.3 fusion.27
  323.9 1.7 all-gather.9.cloned.1.call-done
  325.6 6.3 copy.92
  331.9 20.6 %fusion.38 = bf16[128,2,6,128]{0,3,2,1:T(8,128)(2,1)S(1)} fusion(f32[128,2,6,128]{0,3,2,1:T(8,128)} %fusion.27, bf16[8192,2,128,1]{0,2,3,1:T(8,128)(2,1)} %bitcast.173, f32[2,8192,128,6]{2,1,3,0:T(8,128)} %get-tuple-element.11, f32[2,6,128]{2,1,0:T(8,128)S(1)} %get-tuple-element.8, pred[128,8192]{0,1:T(8,128)(4,1)S(1)} %fusion.13, ...), kind=kOutput, calls=%fused_computation.39 | convolution fusion | flops 3284729856 | bytes 56766464 | tf_op jit(solution)/shard_map/grtk,kgd->grtd/dot_general | solution.py:34
  352.6 3.2 multiply_reduce_fusion.1
  355.9 0.9 copy-done.1
  356.7 0.1 multiply_convert_fusion
  356.9 0.7 copy-done.5
  357.6 0.4 broadcast_in_dim.82
  358.0 1.4 reshape.279
  359.4 4.8 scatter_custom_fusion
  364.1 0.4 broadcast_in_dim.83
  364.5 114.2 %all_to_all.15 = bf16[64,1,24,1536]{3,2,1,0:T(8,128)(2,1)S(1)} all-to-all(bf16[64,1,24,1536]{3,2,1,0:T(8,128)(2,1)S(1)} %bitcast.166), channel_id=1, replica_groups=mesh['tok'=64,'grp'=4] {'tok'}, dimensions={0} | all-to-all | bytes 9437184 | tf_op jit(solution)/shard_map/all_to_all | solution.py:127
  478.7 2.2 copy-done.3
  480.9 4.0 convolution_maximum_fusion
  484.9 8.6 %convolution_convert_fusion = bf16[1536,1536]{1,0:T(8,128)(2,1)} fusion(bf16[1,384,1536]{2,1,0:T(8,128)(2,1)S(1)} %copy-done, f32[1536,384]{1,0:T(8,128)} %convolution_maximum_fusion, bf16[1536,1536]{1,0:T(8,128)(2,1)} %bitcast.171, bf16[1,1536,384]{2,1,0:T(8,128)(2,1)S(1)} %copy-done.14), kind=kOutput, calls=%fused_computation.15 | convolution fusion | flops 3627417600 | bytes 14155776 | tf_op jit(solution)/shard_map/dot_general | solution.py:137
  493.5 6.3 all-to-all-start.2
  499.8 0.1 copy.99
  500.0 0.1 reshape.269
  500.1 0.2 fusion.59
  500.3 3.8 gather_fusion.1
  504.1 0.1 reshape.272
  504.2 0.1 copy.100
  504.3 0.1 copy.101
  504.4 102.9 %all-to-all-done.2 = bf16[64,1,24,1536]{3,2,1,0:T(8,128)(2,1)} async-done(((bf16[64,1,24,1536]{3,2,1,0:T(8,128)(2,1)}), bf16[64,1,24,1536]{3,2,1,0:T(8,128)(2,1)}, u32[]{:S(2)}, u32[]{:S(2)}) %all-to-all-start.2) | async-done | bytes 4718624 | tf_op jit(solution)/shard_map/all_to_all | solution.py:143
  607.4 3.0 bitcast_reduce_fusion.1
  610.4 2.8 convert_element_type.56
  613.2 6.9 %gather_fusion = f32[512,1536]{1,0:T(8,128)} fusion(f32[768,1536]{1,0:T(8,128)} %convert_element_type.56, s32[1024]{0:T(1024)S(1)} %pad_clamp_fusion), kind=kCustom, calls=%fused_computation | custom fusion | bytes 6293504 | tf_op jit(solution)/shard_map/gather | solution.py:149
  620.1 4.9 reshape.260
  624.9 4.2 multiply_reduce_fusion
  629.1 1.0 add_bitcast_fusion
  (50 shorter events, 0.3 us)
Async XLA Ops:
  6.5 478.4 %copy-start = (bf16[1,384,1536]{2,1,0:T(8,128)(2,1)S(1)}, bf16[1,384,1536]{2,1,0:T(8,128)(2,1)}, u32[]{:S(2)}) copy-start(bf16[1,384,1536]{2,1,0:T(8,128)(2,1)} %param.27) | copy-start | bytes 3538948
  10.6 14.6 %copy-start.11 = (s32[1,128,4]{1,2,0:T(4,128)S(1)}, s32[1,128,4]{1,2,0:T(4,128)}, u32[]{:S(2)}) copy-start(s32[1,128,4]{1,2,0:T(4,128)} %param.24) | copy-start | bytes 6148
  10.6 15.8 %copy-start.9 = (bf16[1,128,1536]{2,1,0:T(8,128)(2,1)S(1)}, bf16[1,128,1536]{2,1,0:T(8,128)(2,1)}, u32[]{:S(2)}) copy-start(bf16[1,128,1536]{2,1,0:T(8,128)(2,1)} %param.15) | copy-start | bytes 1179652
  10.6 243.7 %all-to-all-start = ((bf16[64,128,256]{1,2,0:T(8,128)(2,1)}), bf16[64,128,256]{1,2,0:T(8,128)(2,1)}, u32[]{:S(2)}, u32[]{:S(2)}) async-start(bf16[64,128,256]{1,2,0:T(8,128)(2,1)} %stack.3), calls=%async_computation | async-start | bytes 8388608 | tf_op jit(solution)/shard_map/all_to_all | solution.py:84
  22.9 115.9 %all-gather.5.cloned.1.call-start = ((), (), s32[]{:S(2)}) async-start(), calls=%async_computation.3 | async-start | bytes 1052672 | tf_op jit(solution)/shard_map/all_gather | solution.py:76
  23.7 221.1 %all-gather.7.cloned.1.call-start = ((), (), s32[]{:S(2)}) async-start(), calls=%async_computation.4 | async-start | bytes 1052672 | tf_op jit(solution)/shard_map/all_gather | solution.py:77
  24.4 301.2 %all-gather.9.cloned.1.call-start = ((), (), s32[]{:S(2)}) async-start(), calls=%async_computation.5 | async-start | bytes 4259840 | tf_op jit(solution)/shard_map/all_gather | solution.py:86
  261.2 7.4 %copy-start.7 = (bf16[1,128,1536]{1,2,0:T(8,128)(2,1)S(1)}, bf16[1,128,1536]{1,2,0:T(8,128)(2,1)}, u32[]{:S(2)}) copy-start(bf16[1,128,1536]{1,2,0:T(8,128)(2,1)} %copy.82) | copy-start | bytes 1179652
  289.9 30.6 %slice-start = ((s8[12582912]{0:T(1024)(128)(4,1)}), s8[4194304]{0:T(1024)(128)(4,1)S(1)}, s32[]{:S(2)}) async-start(s8[12582912]{0:T(1024)(128)(4,1)} %bitcast.164), calls=%async_computation.6 | async-start | bytes 8388608
  296.7 23.8 %slice-start.1 = ((s8[12582912]{0:T(1024)(128)(4,1)}), s8[4194304]{0:T(1024)(128)(4,1)S(1)}, s32[]{:S(2)}) async-start(s8[12582912]{0:T(1024)(128)(4,1)} %bitcast.164), calls=%async_computation.7 | async-start | bytes 8388608
  296.7 23.8 %slice-start.2 = ((s8[12582912]{0:T(1024)(128)(4,1)}), s8[4194304]{0:T(1024)(128)(4,1)S(1)}, s32[]{:S(2)}) async-start(s8[12582912]{0:T(1024)(128)(4,1)} %bitcast.164), calls=%async_computation.8 | async-start | bytes 8388608
  296.8 23.8 %copy-start.4 = (bf16[2048,256]{0,1:T(8,128)(2,1)S(1)}, bf16[2048,256]{0,1:T(8,128)(2,1)}, u32[]{:S(2)}) copy-start(bf16[2048,256]{0,1:T(8,128)(2,1)} %copy.85) | copy-start | bytes 3145732
  331.9 20.6 %copy-start.8 = (f32[1,128,1536]{2,1,0:T(8,128)S(1)}, f32[1,128,1536]{2,1,0:T(8,128)}, u32[]{:S(2)}) copy-start(f32[1,128,1536]{2,1,0:T(8,128)} %param.14) | copy-start | bytes 2359300
  352.6 4.1 copy-start.12
  355.8 0.9 copy-start.1
  356.9 0.7 copy-start.5
  364.5 116.3 %copy-start.13 = (bf16[1,1536,384]{2,1,0:T(8,128)(2,1)S(1)}, bf16[1,1536,384]{2,1,0:T(8,128)(2,1)}, u32[]{:S(2)}) copy-start(bf16[1,1536,384]{2,1,0:T(8,128)(2,1)} %param.25) | copy-start | bytes 3538948
  478.7 2.2 copy-start.3
  480.9 4.0 copy-start.14
  493.5 6.6 %copy-start.6 = (bf16[128,1536]{1,0:T(8,128)(2,1)S(1)}, bf16[128,1536]{1,0:T(8,128)(2,1)}, u32[]{:S(2)}) copy-start(bf16[128,1536]{1,0:T(8,128)(2,1)} %copy-done.5) | copy-start | bytes 1179652
  493.5 6.6 %copy-start.10 = (bf16[1536,32]{0,1:T(8,128)(2,1)S(1)}, bf16[1536,32]{0,1:T(8,128)(2,1)}, u32[]{:S(2)}) copy-start(bf16[1536,32]{0,1:T(8,128)(2,1)} %param.23) | copy-start | bytes 294916
  493.5 113.9 %all-to-all-start.2 = ((bf16[64,1,24,1536]{3,2,1,0:T(8,128)(2,1)}), bf16[64,1,24,1536]{3,2,1,0:T(8,128)(2,1)}, u32[]{:S(2)}, u32[]{:S(2)}) async-start(bf16[64,1,24,1536]{3,2,1,0:T(8,128)(2,1)} %bitcast.169), calls=%async_computation.2 | async-start | bytes 9437184 | tf_op jit(solution)/shard_map/all_to_all | solution.py:143
  620.1 9.0 %copy-start.2 = (f32[128,1536]{1,0:T(8,128)S(1)}, f32[128,1536]{1,0:T(8,128)}, u32[]{:S(2)}) copy-start(f32[128,1536]{1,0:T(8,128)} %copy-done.1) | copy-start | bytes 2359300
Sparse Core Ops, SparseCore 0:
  27.5 111.3 all-gather.4
  142.6 102.0 all-gather.6
  247.5 78.0 all-gather.8
